TPU v7x, 32 devices: a whole 2x2x4 slice. The times are simulated.
32 devices in a mesh: section: 4 (over y, x), fsdp: 8 (over z, core).
Axes of the slice: x: 2, y: 2, z: 4, core: 2. Of those that a mesh axis runs over, the one named last changes fastest.
Arguments:
- residual_input: bfloat16 [2, 512, 8192], P(None, 'fsdp'), may hold values from -6 to 6
- output_gradient: bfloat16 [2, 512, 8192], P(None, 'fsdp'), may hold values from -0.01953125 to 0.01953125
- value_projection_weight: bfloat16 [4, 8192, 512], P('section', 'fsdp'), may hold values from -0.0625 to 0.0625
- output_weight: bfloat16 [4, 512, 8192], P('section', None, 'fsdp'), may hold values from -0.25 to 0.25
- adapter_down_weight: bfloat16 [4, 8192, 160], P('section'), may hold values from -0.0625 to 0.0625
- adapter_up_weight: bfloat16 [4, 160, 512], P('section'), may hold values from -0.625 to 0.625
- input_norm_scale: float32 [4, 8192], P('section'), may hold values from 0.25 to 1.75
- segment_adapter_index: int32 [2, 16], P(None, 'fsdp'), may hold values from 0 to 3
- adapter_rank_blocks: int32 [4], replicated, may hold values from 1 to 16, 20 in all
Outputs:
- grad_down: float32 [4, 8192, 160], P('section', 'fsdp')
- grad_up: float32 [4, 160, 512], P('section', None, 'fsdp')
Inputs may be any that keep to these rules, and one draw needn't show every extreme that they name: `segment_adapter_index`: adapter of each block of 32 consecutive tokens. `adapter_rank_blocks`: the entries sum to 20.
All inputs are finite; a program needn't handle non-finite values.
Results may differ from a plain program's by a relative error of at most 0.014.
Values may be sent and summed in bfloat16 or wider, within the bound.
A program may use at most 128 MiB of HBM per device.

v0:
```python
import jax
import jax.numpy as jnp
from jax import lax
from jax.sharding import PartitionSpec as P

ADAPTERS = 4
SEG = 32
PACKED_COLUMNS = 160


EPSILON = 1e-06
ADAPTER_ALPHA = 32.0


def from_behind(value, axis, steps):
    count = lax.axis_size(axis)
    leading, last = (max(0, -steps), min(count, count - steps))
    return lax.ppermute(value, axis, [(source, source + steps) for source in range(leading, last)])


def coefficients(segments, adapter_rank_blocks):
    rank_sizes = 8 * adapter_rank_blocks
    rank_ends = jnp.cumsum(rank_sizes)
    columns = jnp.arange(PACKED_COLUMNS, dtype=jnp.int32)
    column_owner = jnp.sum((columns[:, None] >= rank_ends[None, :]).astype(jnp.int32), axis=1)
    token_adapter = jnp.repeat(segments, SEG)
    selector = (token_adapter[:, None] == jnp.arange(ADAPTERS, dtype=jnp.int32)[None, :]).astype(
        jnp.float32
    )
    token_rank_mask = jnp.sum(selector * rank_sizes.astype(jnp.float32)[None, :], axis=1)
    adapter_matches = (token_adapter[:, None] == column_owner[None, :]).astype(jnp.float32)
    return adapter_matches * (ADAPTER_ALPHA / token_rank_mask)[:, None]


def section_forward_pass(
    layer_activation,
    norm_gains,
    value_weight,
    out_weight,
    down_matrix,
    up_matrix,
    scale_coefficient,
):
    widened = layer_activation.astype(jnp.float32)
    inverse_root_mean = lax.rsqrt(jnp.mean(widened * widened, axis=-1) + EPSILON)
    normalized_input = (widened * inverse_root_mean[:, None] * norm_gains[None, :]).astype(
        jnp.bfloat16
    )
    rank_projection = (
        jnp.dot(normalized_input, down_matrix, preferred_element_type=jnp.float32)
        * scale_coefficient
    ).astype(jnp.bfloat16)
    value = (
        jnp.dot(normalized_input, value_weight, preferred_element_type=jnp.float32)
        + jnp.dot(rank_projection, up_matrix, preferred_element_type=jnp.float32)
    ).astype(jnp.bfloat16)
    section_output = (
        widened + jnp.dot(value, out_weight, preferred_element_type=jnp.float32)
    ).astype(jnp.bfloat16)
    return (section_output, normalized_input, rank_projection, inverse_root_mean)


def contract(left, right, left_dim, right_dim):
    return lax.dot_general(
        left, right, (((left_dim,), (right_dim,)), ((), ())), preferred_element_type=jnp.float32
    )


def section_backward_pass(
    layer_activation,
    incoming_gradient,
    norm_gains,
    value_weight,
    out_weight,
    down_matrix,
    up_matrix,
    scale_coefficient,
    inverse_root_mean,
):
    value_grad = contract(incoming_gradient, out_weight, 1, 1).astype(jnp.bfloat16)
    low_grad = (contract(value_grad, up_matrix, 1, 1) * scale_coefficient).astype(jnp.bfloat16)
    normed_grad = contract(value_grad, value_weight, 1, 1) + contract(low_grad, down_matrix, 1, 1)
    widened = layer_activation.astype(jnp.float32)
    scaled = normed_grad * norm_gains[None, :]
    cubed = inverse_root_mean * inverse_root_mean * inverse_root_mean
    input_grad = (
        incoming_gradient.astype(jnp.float32)
        + inverse_root_mean[:, None] * scaled
        - widened * cubed[:, None] * jnp.mean(widened * scaled, axis=-1, keepdims=True)
    )
    return (input_grad.astype(jnp.bfloat16), low_grad, value_grad)


def remember(stash, item, batch_slot, active):
    previous = lax.dynamic_index_in_dim(stash, batch_slot, 0, keepdims=False)
    return lax.dynamic_update_index_in_dim(stash, jnp.where(active, item, previous), batch_slot, 0)


def recall(stash, batch_slot):
    return lax.dynamic_index_in_dim(stash, batch_slot, 0, keepdims=False)


def local(
    residual_input,
    output_gradient,
    value_projection_weight,
    output_weight,
    adapter_down_weight,
    adapter_up_weight,
    input_norm_scale,
    segment_adapter_index,
    adapter_rank_blocks,
):
    section_count = lax.axis_size("section")
    section_index = lax.axis_index("section")
    micro_count = residual_input.shape[0]
    rows = residual_input.shape[1]
    value_full = lax.all_gather(value_projection_weight[0], "fsdp", axis=0, tiled=True)
    out_full = lax.all_gather(output_weight[0], "fsdp", axis=1, tiled=True)
    down_matrix = adapter_down_weight[0]
    up_matrix = adapter_up_weight[0]
    norm_gains = input_norm_scale[0]
    coef_table = jnp.stack(
        [
            coefficients(segment_adapter_index[which], adapter_rank_blocks)
            for which in range(micro_count)
        ]
    )
    ticks = micro_count + section_count - 1
    packed = down_matrix.shape[1]
    width = down_matrix.shape[0]
    value_cols = up_matrix.shape[1]
    inputs_kept = jnp.zeros_like(residual_input)
    normed_kept = jnp.zeros_like(residual_input)
    low_kept = jnp.zeros((micro_count, rows, packed), jnp.bfloat16)
    rms_kept = jnp.zeros((micro_count, rows), jnp.float32)
    received = jnp.zeros_like(residual_input[0])
    for moment in range(ticks):
        micro_index = moment - section_index
        active = (micro_index >= 0) & (micro_index < micro_count)
        batch_slot = jnp.clip(micro_index, 0, micro_count - 1)
        section_input = jnp.where(
            section_index == 0, residual_input[min(moment, micro_count - 1)], received
        )
        scale_coefficient = recall(coef_table, batch_slot)
        section_output, normalized_input, rank_projection, inverse_root_mean = section_forward_pass(
            section_input,
            norm_gains,
            value_full,
            out_full,
            down_matrix,
            up_matrix,
            scale_coefficient,
        )
        inputs_kept = remember(inputs_kept, section_input, batch_slot, active)
        normed_kept = remember(normed_kept, normalized_input, batch_slot, active)
        low_kept = remember(low_kept, rank_projection, batch_slot, active)
        rms_kept = remember(rms_kept, inverse_root_mean, batch_slot, active)
        if moment + 1 < ticks:
            received = from_behind(section_output, "section", 1)
    low_grad_kept = jnp.zeros((micro_count, rows, packed), jnp.bfloat16)
    value_grad_kept = jnp.zeros((micro_count, rows, value_cols), jnp.bfloat16)
    grad_received = jnp.zeros_like(residual_input[0])
    for moment in range(ticks):
        micro_index = moment - (section_count - 1 - section_index)
        active = (micro_index >= 0) & (micro_index < micro_count)
        batch_slot = jnp.clip(micro_index, 0, micro_count - 1)
        incoming_gradient = jnp.where(
            section_index == section_count - 1,
            output_gradient[min(moment, micro_count - 1)],
            grad_received,
        )
        scale_coefficient = recall(coef_table, batch_slot)
        layer_activation = recall(inputs_kept, batch_slot)
        normalized_input = recall(normed_kept, batch_slot)
        rank_projection = recall(low_kept, batch_slot)
        inverse_root_mean = recall(rms_kept, batch_slot)
        input_grad, low_grad, value_grad = section_backward_pass(
            layer_activation,
            incoming_gradient,
            norm_gains,
            value_full,
            out_full,
            down_matrix,
            up_matrix,
            scale_coefficient,
            inverse_root_mean,
        )
        input_grad, low_grad, value_grad, normed_used, rank_used = (
            input_grad,
            low_grad,
            value_grad,
            normalized_input,
            rank_projection,
        )
        low_grad_kept = remember(low_grad_kept, low_grad, batch_slot, active)
        value_grad_kept = remember(value_grad_kept, value_grad, batch_slot, active)
        if moment + 1 < ticks:
            grad_received = from_behind(input_grad, "section", -1)
    all_rows = micro_count * rows
    up_sum = contract(
        low_kept.reshape(all_rows, packed), value_grad_kept.reshape(all_rows, value_cols), 0, 0
    )
    down_sum = contract(
        normed_kept.reshape(all_rows, width), low_grad_kept.reshape(all_rows, packed), 0, 0
    )
    down_part, up_part = (
        lax.psum_scatter(down_sum, "fsdp", scatter_dimension=0, tiled=True),
        lax.psum_scatter(up_sum, "fsdp", scatter_dimension=1, tiled=True),
    )
    return (down_part[None], up_part[None])


def solution(mesh):
    placed = (
        P(None, "fsdp", None),
        P(None, "fsdp", None),
        P("section", "fsdp", None),
        P("section", None, "fsdp"),
        P("section", None, None),
        P("section", None, None),
        P("section", None),
        P(None, "fsdp"),
        P(),
    )
    return jax.shard_map(
        local,
        mesh=mesh,
        in_specs=placed,
        out_specs=(P("section", "fsdp", None), P("section", None, "fsdp")),
        check_vma=False,
    )
```

profile of v0, /device:TPU:0, one launch (start us, length us, event | category | flops | bytes accessed | tf_op | source)
XLA Modules:
  0.0 584.1 jit_solution(9267205419562154387)
XLA Ops:
  9.3 1.6 fusion.54
  11.3 2.3 bitcast_dynamic-update-slice_fusion.16
  13.6 1.6 broadcast.377.clone
  17.2 2.3 constant_dynamic-slice_fusion.18
  19.5 74.9 %all-gather.5.cloned.1.call-done = bf16[1,8192,512]{2,1,0:T(8,128)(2,1)} async-done(((bf16[1,1024,512]{2,1,0:T(8,128)(2,1)}), bf16[1,8192,512]{2,1,0:T(8,128)(2,1)}) %all-gather.5.cloned.1.call-update) | async-done | bytes 8388624 | tf_op jit(solution)/shard_map/all_gather | solution.py:118
  94.4 5.3 fusion.32
  99.7 76.8 %all-gather.7.cloned.1.call-done = bf16[1,512,8192]{2,1,0:T(8,128)(2,1)} async-done(((bf16[1,512,1024]{2,1,0:T(8,128)(2,1)}), bf16[1,512,8192]{2,1,0:T(8,128)(2,1)}) %all-gather.7.cloned.1.call-update) | async-done | bytes 8388624 | tf_op jit(solution)/shard_map/all_gather | solution.py:119
  176.6 6.3 %fusion.4 = bf16[64,8192]{1,0:T(8,128)(2,1)} fusion(bf16[1,512,8192]{2,1,0:T(8,128)(2,1)} %all-gather.7.cloned.1.call-done, f32[64,512]{1,0:T(8,128)S(1)} %fusion.32, bf16[64,160]{1,0:T(8,128)(2,1)S(1)} %get-tuple-element.52, bf16[1,160,512]{2,1,0:T(8,128)(2,1)S(1)} %copy-done.16, bf16[2,64,8192]{2,1,0:T(8,128)(2,1)} %param.9, pred[]{:T(512)S(6)} %eq.82), kind=kOutput, calls=%fused_computation.13 | convolution fusion | flops 549519360 | bytes 10801153 | tf_op jit(solution)/shard_map/dot_general | solution.py:58
  182.9 3.4 collective-permute-start
  186.3 6.4 %bitcast_dynamic-update-slice_fusion.12 = (bf16[2,64,512]{2,1,0:T(8,128)(2,1)S(1)}, bf16[64,512]{1,0:T(8,128)(2,1)S(1)}) fusion(bf16[2,64,512]{2,1,0:T(8,128)(2,1)S(1)} %broadcast_in_dim.149, s32[]{:T(128)S(6)} %min.36, pred[]{:T(512)S(6)} %and.36, bf16[1,512,8192]{2,1,0:T(8,128)(2,1)} %all-gather.7.cloned.1.call-done, bf16[2,64,8192]{2,1,0:T(8,128)(2,1)} %param.10, ...), kind=kOutput, calls=%fused_computation.249 | convolution fusion | flops 537460736 | bytes 9568262 | tf_op jit(solution)/shard_map/dot_general | solution.py:64
  193.0 1.9 fusion.44
  194.8 14.5 %collective-permute-done = bf16[64,8192]{1,0:T(8,128)(2,1)S(1)} collective-permute-done((bf16[64,8192]{1,0:T(8,128)(2,1)}, bf16[64,8192]{1,0:T(8,128)(2,1)S(1)}, u32[]{:S(2)}, u32[]{:S(2)}) %collective-permute-start) | collective-permute-done | bytes 1048608 | tf_op jit(solution)/shard_map/ppermute | solution.py:18
  212.3 10.4 %fusion.5 = bf16[64,8192]{1,0:T(8,128)(2,1)} fusion(bf16[1,512,8192]{2,1,0:T(8,128)(2,1)} %all-gather.7.cloned.1.call-done, bf16[64,8192]{1,0:T(8,128)(2,1)} %copy-done.12, f32[64,512]{1,0:T(8,128)S(1)} %fusion.193, bf16[1,8192,512]{2,1,0:T(8,128)(2,1)} %all-gather.5.cloned.1.call-done, f32[64]{0:T(128)S(1)} %add_rsqrt_fusion.3, f32[8192]{0:T(1024)S(1)} %bitcast.467), kind=kOutput, calls=%fused_computation.14 | convolution fusion | flops 1077477376 | bytes 19038464 | tf_op jit(solution)/shard_map/dot_general | solution.py:58
  222.7 5.3 collective-permute-start.1
  229.7 19.6 %collective-permute-done.1 = bf16[64,8192]{1,0:T(8,128)(2,1)} collective-permute-done((bf16[64,8192]{1,0:T(8,128)(2,1)}, bf16[64,8192]{1,0:T(8,128)(2,1)}, u32[]{:S(2)}, u32[]{:S(2)}) %collective-permute-start.1) | collective-permute-done | bytes 1048608 | tf_op jit(solution)/shard_map/ppermute | solution.py:18
  252.2 10.4 %fusion.6 = bf16[64,8192]{1,0:T(8,128)(2,1)} fusion(bf16[1,512,8192]{2,1,0:T(8,128)(2,1)} %all-gather.7.cloned.1.call-done, bf16[64,8192]{1,0:T(8,128)(2,1)} %copy-done.14, f32[64,512]{1,0:T(8,128)S(1)} %fusion.191, bf16[1,8192,512]{2,1,0:T(8,128)(2,1)} %all-gather.5.cloned.1.call-done, f32[64]{0:T(128)S(1)} %add_rsqrt_fusion.2, f32[8192]{0:T(1024)S(1)} %bitcast.469), kind=kOutput, calls=%fused_computation.15 | convolution fusion | flops 1077477376 | bytes 19038464 | tf_op jit(solution)/shard_map/dot_general | solution.py:58
  262.6 6.6 %collective-permute-start.2 = (bf16[64,8192]{1,0:T(8,128)(2,1)}, bf16[64,8192]{1,0:T(8,128)(2,1)}, u32[]{:S(2)}, u32[]{:S(2)}) collective-permute-start(bf16[64,8192]{1,0:T(8,128)(2,1)} %fusion.6), channel_id=1, source_target_pairs={{0,8},{8,16},{16,24},{1,9},{9,17},{17,25},{2,10},{10,18},{18,26},{... | collective-permute-start | bytes 3145736 | tf_op jit(solution)/shard_map/ppermute | solution.py:18
  270.7 18.9 %collective-permute-done.2 = bf16[64,8192]{1,0:T(8,128)(2,1)} collective-permute-done((bf16[64,8192]{1,0:T(8,128)(2,1)}, bf16[64,8192]{1,0:T(8,128)(2,1)}, u32[]{:S(2)}, u32[]{:S(2)}) %collective-permute-start.2) | collective-permute-done | bytes 1048608 | tf_op jit(solution)/shard_map/ppermute | solution.py:18
  292.6 10.5 %fusion.7 = bf16[64,8192]{1,0:T(8,128)(2,1)} fusion(bf16[1,512,8192]{2,1,0:T(8,128)(2,1)} %all-gather.7.cloned.1.call-done, bf16[64,8192]{1,0:T(8,128)(2,1)} %copy-done.10, f32[64,512]{1,0:T(8,128)S(1)} %fusion.189, bf16[1,8192,512]{2,1,0:T(8,128)(2,1)} %all-gather.5.cloned.1.call-done, f32[64]{0:T(128)S(1)} %add_rsqrt_fusion.1, f32[8192]{0:T(1024)S(1)} %bitcast.471), kind=kOutput, calls=%fused_computation.16 | convolution fusion | flops 1077477376 | bytes 19038464 | tf_op jit(solution)/shard_map/dot_general | solution.py:58
  303.1 7.4 %collective-permute-start.3 = (bf16[64,8192]{1,0:T(8,128)(2,1)}, bf16[64,8192]{1,0:T(8,128)(2,1)}, u32[]{:S(2)}, u32[]{:S(2)}) collective-permute-start(bf16[64,8192]{1,0:T(8,128)(2,1)} %fusion.7), channel_id=1, source_target_pairs={{0,8},{8,16},{16,24},{1,9},{9,17},{17,25},{2,10},{10,18},{18,26},{... | collective-permute-start | bytes 3145736 | tf_op jit(solution)/shard_map/ppermute | solution.py:18
  310.5 1.4 constant_dynamic-slice_fusion.15
  312.0 18.1 %collective-permute-done.3 = bf16[64,8192]{1,0:T(8,128)(2,1)} collective-permute-done((bf16[64,8192]{1,0:T(8,128)(2,1)}, bf16[64,8192]{1,0:T(8,128)(2,1)}, u32[]{:S(2)}, u32[]{:S(2)}) %collective-permute-start.3) | collective-permute-done | bytes 1048608 | tf_op jit(solution)/shard_map/ppermute | solution.py:18
  330.3 1.9 bitcast_dynamic-update-slice_fusion
  334.9 7.2 %fusion.65 = (f32[64]{0:T(128)S(1)}, f32[64,8192]{1,0:T(8,128)S(1)}) fusion(bf16[2,64,8192]{2,1,0:T(8,128)(2,1)} %get-tuple-element.12, s32[]{:T(128)S(6)} %min.36, f32[8192]{0:T(1024)S(1)} %bitcast.473, f32[64,8192]{1,0:T(8,128)} %fusion.44, bf16[64,512]{1,0:T(8,128)(2,1)S(1)} %get-tuple-element.60, bf16[1,8192,512]{2,1,0:T(8,128)(2,1)} %all-gather.5.cloned.1.call-done), kind=kOutput, calls=%fused_computation.92 | convolution fusion | flops 539492288 | bytes 13730052 | tf_op jit(solution)/shard_map/dot_general | solution.py:64
  342.1 2.0 fusion.64
  344.2 1.6 collective-permute-start.4
  347.7 23.2 %collective-permute-done.4 = bf16[64,8192]{1,0:T(8,128)(2,1)S(1)} collective-permute-done((bf16[64,8192]{1,0:T(8,128)(2,1)S(1)}, bf16[64,8192]{1,0:T(8,128)(2,1)S(1)}, u32[]{:S(2)}, u32[]{:S(2)}) %collective-permute-start.4) | collective-permute-done | bytes 1048608 | tf_op jit(solution)/shard_map/ppermute | solution.py:18
  370.9 2.7 bitcast_dynamic-update-slice_fusion.11
  373.8 1.9 fusion.42
  375.7 6.1 %fusion.69 = (f32[64]{0:T(128)S(1)}, f32[64,8192]{1,0:T(8,128)}) fusion(bf16[2,64,8192]{2,1,0:T(8,128)(2,1)} %get-tuple-element.12, s32[]{:T(128)S(6)} %min.37, f32[8192]{0:T(1024)S(1)} %bitcast.476, f32[64,8192]{1,0:T(8,128)} %fusion.42, bf16[64,512]{1,0:T(8,128)(2,1)S(1)} %get-tuple-element.62, bf16[1,8192,512]{2,1,0:T(8,128)(2,1)S(1)} %bitcast.463), kind=kOutput, calls=%fused_computation.96 | convolution fusion | flops 539492288 | bytes 13730052 | tf_op jit(solution)/shard_map/dot_general | solution.py:64
  381.9 2.6 fusion.68
  385.9 23.4 %collective-permute-done.5 = bf16[64,8192]{1,0:T(8,128)(2,1)S(1)} collective-permute-done((bf16[64,8192]{1,0:T(8,128)(2,1)S(1)}, bf16[64,8192]{1,0:T(8,128)(2,1)S(1)}, u32[]{:S(2)}, u32[]{:S(2)}) %collective-permute-start.5) | collective-permute-done | bytes 1048608 | tf_op jit(solution)/shard_map/ppermute | solution.py:18
  409.3 2.7 bitcast_dynamic-update-slice_fusion.10
  412.1 1.9 fusion.40
  414.0 6.0 %fusion.73 = (f32[64]{0:T(128)S(1)}, f32[64,8192]{1,0:T(8,128)}) fusion(bf16[2,64,8192]{2,1,0:T(8,128)(2,1)} %get-tuple-element.12, s32[]{:T(128)S(6)} %min.38, f32[8192]{0:T(1024)S(1)} %bitcast.477, f32[64,8192]{1,0:T(8,128)} %fusion.40, bf16[64,512]{1,0:T(8,128)(2,1)S(1)} %get-tuple-element.64, bf16[1,8192,512]{2,1,0:T(8,128)(2,1)S(1)} %bitcast.463), kind=kOutput, calls=%fused_computation.100 | convolution fusion | flops 539492288 | bytes 13730052 | tf_op jit(solution)/shard_map/dot_general | solution.py:64
  420.1 3.0 fusion.72
  423.0 1.5 collective-permute-start.6
  425.2 21.1 %collective-permute-done.6 = bf16[64,8192]{1,0:T(8,128)(2,1)S(1)} collective-permute-done((bf16[64,8192]{1,0:T(8,128)(2,1)S(1)}, bf16[64,8192]{1,0:T(8,128)(2,1)S(1)}, u32[]{:S(2)}, u32[]{:S(2)}) %collective-permute-start.6) | collective-permute-done | bytes 1048608 | tf_op jit(solution)/shard_map/ppermute | solution.py:18
  446.3 2.7 bitcast_dynamic-update-slice_fusion.9
  449.1 1.9 fusion.38
  451.0 6.0 %fusion.77 = (f32[64]{0:T(128)S(1)}, f32[64,8192]{1,0:T(8,128)}) fusion(bf16[2,64,8192]{2,1,0:T(8,128)(2,1)} %get-tuple-element.12, s32[]{:T(128)S(6)} %min.39, f32[8192]{0:T(1024)S(1)} %bitcast.479, f32[64,8192]{1,0:T(8,128)} %fusion.38, bf16[64,512]{1,0:T(8,128)(2,1)S(1)} %get-tuple-element.66, bf16[1,8192,512]{2,1,0:T(8,128)(2,1)S(1)} %bitcast.463), kind=kOutput, calls=%fused_computation.104 | convolution fusion | flops 539492288 | bytes 13730052 | tf_op jit(solution)/shard_map/dot_general | solution.py:64
  457.1 3.0 fusion.76
  463.4 19.0 %collective-permute-done.7 = bf16[64,8192]{1,0:T(8,128)(2,1)S(1)} collective-permute-done((bf16[64,8192]{1,0:T(8,128)(2,1)S(1)}, bf16[64,8192]{1,0:T(8,128)(2,1)S(1)}, u32[]{:S(2)}, u32[]{:S(2)}) %collective-permute-start.7) | collective-permute-done | bytes 1048608 | tf_op jit(solution)/shard_map/ppermute | solution.py:18
  482.4 2.7 bitcast_dynamic-update-slice_fusion.8
  486.2 3.0 bitcast_dynamic-update-slice_fusion.4
  489.4 4.8 convolution_bitcast_fusion
  494.2 22.3 %reduce-scatter.5.cloned.1.call-done = f32[160,64]{0,1:T(8,128)} async-done(((f32[160,512]{0,1:T(8,128)}), f32[160,64]{0,1:T(8,128)}) %reduce-scatter.5.cloned.1.call-update) | async-done | bytes 40976 | tf_op jit(solution)/shard_map/reduce_scatter | solution.py:209
  516.5 60.6 %reduce-scatter.3.cloned.1.call-done = f32[1024,160]{0,1:T(8,128)} async-done(((f32[8192,160]{0,1:T(8,128)}), f32[1024,160]{0,1:T(8,128)}) %reduce-scatter.3.cloned.1.call-update) | async-done | bytes 655376 | tf_op jit(solution)/shard_map/reduce_scatter | solution.py:208
  (151 shorter events, 28.5 us)
Async XLA Ops:
  7.2 4.1 copy-start
  7.2 1.6 copy-start.25
  7.2 1.9 copy-start.26
  7.2 4.1 copy-start.19
  7.2 87.2 %all-gather.5.cloned.1.call-start = ((), (), s32[]{:S(2)}) async-start(), calls=%async_computation.4 | async-start | bytes 9437184 | tf_op jit(solution)/shard_map/all_gather | solution.py:118
  7.9 168.6 %all-gather.7.cloned.1.call-start = ((), (), s32[]{:S(2)}) async-start(), calls=%async_computation.5 | async-start | bytes 9437184 | tf_op jit(solution)/shard_map/all_gather | solution.py:119
  8.7 507.8 %reduce-scatter.5.cloned.1.call-start = ((), (), s32[]{:S(2)}) async-start(), calls=%async_computation.3 | async-start | bytes 589824 | tf_op jit(solution)/shard_map/reduce_scatter | solution.py:209
  13.6 2.4 copy-start.1
  19.5 157.1 %copy-start.16 = (bf16[1,160,512]{2,1,0:T(8,128)(2,1)S(1)}, bf16[1,160,512]{2,1,0:T(8,128)(2,1)}, u32[]{:S(2)}) copy-start(bf16[1,160,512]{2,1,0:T(8,128)(2,1)} %param.14) | copy-start | bytes 491524
  182.9 26.5 %collective-permute-start = (bf16[64,8192]{1,0:T(8,128)(2,1)}, bf16[64,8192]{1,0:T(8,128)(2,1)S(1)}, u32[]{:S(2)}, u32[]{:S(2)}) collective-permute-start(bf16[64,8192]{1,0:T(8,128)(2,1)} %fusion.4), channel_id=1, source_target_pairs={{0,8},{8,16},{16,24},{1,9},{9,17},{17,25},{2,10},{10,18},{18,26},{... | collective-permute-start | bytes 3145736 | tf_op jit(solution)/shard_map/ppermute | solution.py:18
  192.9 16.4 %copy-start.2 = (bf16[2,64,8192]{2,1,0:T(8,128)(2,1)S(1)}, bf16[2,64,8192]{2,1,0:T(8,128)(2,1)}, u32[]{:S(2)}) copy-start(bf16[2,64,8192]{2,1,0:T(8,128)(2,1)} %param.9) | copy-start | bytes 6291460
  193.0 16.4 %copy-start.20 = (bf16[1,64,8192]{2,1,0:T(8,128)(2,1)S(1)}, bf16[1,64,8192]{2,1,0:T(8,128)(2,1)}, u32[]{:S(2)}) copy-start(bf16[1,64,8192]{2,1,0:T(8,128)(2,1)} %constant_dynamic-slice_fusion.18) | copy-start | bytes 3145732
  210.8 1.4 copy-start.12
  222.7 26.6 %collective-permute-start.1 = (bf16[64,8192]{1,0:T(8,128)(2,1)}, bf16[64,8192]{1,0:T(8,128)(2,1)}, u32[]{:S(2)}, u32[]{:S(2)}) collective-permute-start(bf16[64,8192]{1,0:T(8,128)(2,1)} %fusion.5), channel_id=1, source_target_pairs={{0,8},{8,16},{16,24},{1,9},{9,17},{17,25},{2,10},{10,18},{18,26},{... | collective-permute-start | bytes 3145736 | tf_op jit(solution)/shard_map/ppermute | solution.py:18
  228.2 21.1 %copy-start.3 = (bf16[2,64,8192]{2,1,0:T(8,128)(2,1)S(1)}, bf16[2,64,8192]{2,1,0:T(8,128)(2,1)}, u32[]{:S(2)}) copy-start(bf16[2,64,8192]{2,1,0:T(8,128)(2,1)} %param.9) | copy-start | bytes 6291460
  250.7 1.4 copy-start.14
  262.6 27.0 %collective-permute-start.2 = (bf16[64,8192]{1,0:T(8,128)(2,1)}, bf16[64,8192]{1,0:T(8,128)(2,1)}, u32[]{:S(2)}, u32[]{:S(2)}) collective-permute-start(bf16[64,8192]{1,0:T(8,128)(2,1)} %fusion.6), channel_id=1, source_target_pairs={{0,8},{8,16},{16,24},{1,9},{9,17},{17,25},{2,10},{10,18},{18,26},{... | collective-permute-start | bytes 3145736 | tf_op jit(solution)/shard_map/ppermute | solution.py:18
  269.3 20.4 %copy-start.4 = (bf16[2,64,8192]{2,1,0:T(8,128)(2,1)S(1)}, bf16[2,64,8192]{2,1,0:T(8,128)(2,1)}, u32[]{:S(2)}) copy-start(bf16[2,64,8192]{2,1,0:T(8,128)(2,1)} %param.9) | copy-start | bytes 6291460
  291.0 1.4 copy-start.10
  303.1 27.0 %collective-permute-start.3 = (bf16[64,8192]{1,0:T(8,128)(2,1)}, bf16[64,8192]{1,0:T(8,128)(2,1)}, u32[]{:S(2)}, u32[]{:S(2)}) collective-permute-start(bf16[64,8192]{1,0:T(8,128)(2,1)} %fusion.7), channel_id=1, source_target_pairs={{0,8},{8,16},{16,24},{1,9},{9,17},{17,25},{2,10},{10,18},{18,26},{... | collective-permute-start | bytes 3145736 | tf_op jit(solution)/shard_map/ppermute | solution.py:18
  310.5 19.7 %copy-start.5 = (bf16[2,64,8192]{2,1,0:T(8,128)(2,1)S(1)}, bf16[2,64,8192]{2,1,0:T(8,128)(2,1)}, u32[]{:S(2)}) copy-start(bf16[2,64,8192]{2,1,0:T(8,128)(2,1)} %param.9) | copy-start | bytes 6291460
  332.2 1.3 copy-start.6
  333.5 1.0 copy-start.17
  334.8 7.3 %copy-start.9 = (bf16[2,64,8192]{2,1,0:T(8,128)(2,1)S(1)}, bf16[2,64,8192]{2,1,0:T(8,128)(2,1)}, u32[]{:S(2)}) copy-start(bf16[2,64,8192]{2,1,0:T(8,128)(2,1)} %param.10) | copy-start | bytes 6291460
  334.9 11.0 %copy-start.7 = (bf16[2,64,8192]{2,1,0:T(8,128)(2,1)S(1)}, bf16[2,64,8192]{2,1,0:T(8,128)(2,1)}, u32[]{:S(2)}) copy-start(bf16[2,64,8192]{2,1,0:T(8,128)(2,1)} %copy-done.6) | copy-start | bytes 6291460
  342.1 28.8 %slice-start = ((s8[8388608]{0:T(1024)(128)(4,1)}), s8[4194304]{0:T(1024)(128)(4,1)S(1)}, s32[]{:S(2)}) async-start(s8[8388608]{0:T(1024)(128)(4,1)} %bitcast.460), calls=%async_computation.6 | async-start | bytes 8388608
  344.1 1.8 copy-start.13
  344.2 26.8 %collective-permute-start.4 = (bf16[64,8192]{1,0:T(8,128)(2,1)S(1)}, bf16[64,8192]{1,0:T(8,128)(2,1)S(1)}, u32[]{:S(2)}, u32[]{:S(2)}) collective-permute-start(bf16[64,8192]{1,0:T(8,128)(2,1)S(1)} %fusion.64), channel_id=1, source_target_pairs={{8,0},{16,8},{24,16},{9,1},{17,9},{25,17},{10,2},{18,10},{26,18},{... | collective-permute-start | bytes 3145736 | tf_op jit(solution)/shard_map/ppermute | solution.py:18
  345.9 1.2 copy-start.15
  345.9 25.0 %slice-start.1 = ((s8[8388608]{0:T(1024)(128)(4,1)}), s8[4194304]{0:T(1024)(128)(4,1)S(1)}, s32[]{:S(2)}) async-start(s8[8388608]{0:T(1024)(128)(4,1)} %bitcast.460), calls=%async_computation.7 | async-start | bytes 8388608
  347.1 28.6 %slice-start.2 = ((s8[8388608]{0:T(1024)(128)(4,1)}), s8[4194304]{0:T(1024)(128)(4,1)S(1)}, s32[]{:S(2)}) async-start(s8[8388608]{0:T(1024)(128)(4,1)} %bitcast.462), calls=%async_computation.8 | async-start | bytes 8388608
  347.7 28.0 %slice-start.3 = ((s8[8388608]{0:T(1024)(128)(4,1)}), s8[4194304]{0:T(1024)(128)(4,1)S(1)}, s32[]{:S(2)}) async-start(s8[8388608]{0:T(1024)(128)(4,1)} %bitcast.462), calls=%async_computation.9 | async-start | bytes 8388608
  370.9 2.7 copy-start.21
  375.7 6.2 %copy-start.22 = (bf16[64,8192]{1,0:T(8,128)(2,1)S(1)}, bf16[64,8192]{1,0:T(8,128)(2,1)}, u32[]{:S(2)}) copy-start(bf16[64,8192]{1,0:T(8,128)(2,1)} %copy-done.21) | copy-start | bytes 3145732
  384.4 24.8 %collective-permute-start.5 = (bf16[64,8192]{1,0:T(8,128)(2,1)S(1)}, bf16[64,8192]{1,0:T(8,128)(2,1)S(1)}, u32[]{:S(2)}, u32[]{:S(2)}) collective-permute-start(bf16[64,8192]{1,0:T(8,128)(2,1)S(1)} %fusion.68), channel_id=1, source_target_pairs={{8,0},{16,8},{24,16},{9,1},{17,9},{25,17},{10,2},{18,10},{26,18},{... | collective-permute-start | bytes 3145736 | tf_op jit(solution)/shard_map/ppermute | solution.py:18
  409.3 2.7 copy-start.24
  420.1 4.5 copy-start.11
  423.0 23.2 %collective-permute-start.6 = (bf16[64,8192]{1,0:T(8,128)(2,1)S(1)}, bf16[64,8192]{1,0:T(8,128)(2,1)S(1)}, u32[]{:S(2)}, u32[]{:S(2)}) collective-permute-start(bf16[64,8192]{1,0:T(8,128)(2,1)S(1)} %fusion.72), channel_id=1, source_target_pairs={{8,0},{16,8},{24,16},{9,1},{17,9},{25,17},{10,2},{18,10},{26,18},{... | collective-permute-start | bytes 3145736 | tf_op jit(solution)/shard_map/ppermute | solution.py:18
  425.1 37.2 %copy-start.8 = (bf16[2,64,8192]{2,1,0:T(8,128)(2,1)}, bf16[2,64,8192]{2,1,0:T(8,128)(2,1)S(1)}, u32[]{:S(2)}) copy-start(bf16[2,64,8192]{2,1,0:T(8,128)(2,1)S(1)} %bitcast_dynamic-update-slice_fusion.5) | copy-start | bytes 6291460
  446.3 2.7 copy-start.23
  457.0 4.3 copy-start.18
  460.0 22.4 %collective-permute-start.7 = (bf16[64,8192]{1,0:T(8,128)(2,1)S(1)}, bf16[64,8192]{1,0:T(8,128)(2,1)S(1)}, u32[]{:S(2)}, u32[]{:S(2)}) collective-permute-start(bf16[64,8192]{1,0:T(8,128)(2,1)S(1)} %fusion.76), channel_id=1, source_target_pairs={{8,0},{16,8},{24,16},{9,1},{17,9},{25,17},{10,2},{18,10},{26,18},{... | collective-permute-start | bytes 3145736 | tf_op jit(solution)/shard_map/ppermute | solution.py:18
  486.2 90.9 %reduce-scatter.3.cloned.1.call-start = ((), (), s32[]{:S(2)}) async-start(), calls=%async_computation.2 | async-start | bytes 5898240 | tf_op jit(solution)/shard_map/reduce_scatter | solution.py:208
Sparse Core Ops, SparseCore 0:
  9.6 84.7 all-gather.4
  96.0 80.5 all-gather.6
  486.3 30.1 reduce-scatter.4
  519.2 57.8 reduce-scatter.2
where the time goes:
time: 592 us; the launch traced here: 584 us
  waiting for transfers between devices  394 us (67%)
  matrix products  107 us (18%)
  starting transfers between devices  28.7 us (5%)
  other arithmetic  25.8 us (4%)
  between operations  15 us (3%)
  local copies, waits for them, and re-layouts  14.2 us (2%)
    ppermute x8, waiting for transfers between devices, from_behind(): lax.ppermute(value, axis, [(source, source + steps) for source in range(l...  158 us
    all_gather x1, waiting for transfers between devices, local(): out_full = lax.all_gather(output_weight[0], 'fsdp', axis=1, tiled=True)  76.8 us
    all_gather x1, waiting for transfers between devices, local(): lax.all_gather(value_projection_weight[0], 'fsdp', axis=0, tiled=True)  74.9 us
    reduce_scatter x1, waiting for transfers between devices, local(): lax.psum_scatter(down_sum, 'fsdp', scatter_dimension=0, tiled=True)  60.6 us
    dot_general x20, matrix products, contract(): lax.dot_general(left, right, (((left_dim,), (right_dim,)), ((), ())), pre...  56.8 us
    dot_general x4, matrix products, section_forward_pass(): jnp.dot(value, out_weight, preferred_element_type=jnp.float32)  37.7 us
    ppermute x8, starting transfers between devices, from_behind(): lax.ppermute(value, axis, [(source, source + steps) for source in range(l...  28.5 us
    reduce_scatter x1, waiting for transfers between devices, local(): lax.psum_scatter(up_sum, 'fsdp', scatter_dimension=1, tiled=True)  22.3 us
  transfers between devices with their start and end apart: 12, of which 12 were waited for; matrix products, arithmetic and copies ran while one was open for 7% of the time, Pallas kernels for 0%

commit v1 on v0

v1 whole, which is shorter than its diff:
```python
import functools

import jax
import jax.numpy as jnp
from jax import lax
from jax.experimental import pallas as pl
from jax.experimental.pallas import tpu as pltpu
from jax.sharding import PartitionSpec as P

SEG = 32
EPSILON = 1e-06
ADAPTER_ALPHA = 32.0
LANES = 128
MESH = pl.DeviceIdType.MESH
F32 = jnp.float32
BF16 = jnp.bfloat16


def coefficients(segments, adapter_rank_blocks, columns_padded):
    adapters = adapter_rank_blocks.shape[0]
    rank_sizes = 8 * adapter_rank_blocks
    rank_ends = jnp.cumsum(rank_sizes)
    columns = jnp.arange(columns_padded, dtype=jnp.int32)
    column_owner = jnp.sum((columns[:, None] >= rank_ends[None, :]).astype(jnp.int32), axis=1)
    token_adapter = jnp.repeat(segments, SEG)
    selector = (token_adapter[:, None] == jnp.arange(adapters, dtype=jnp.int32)[None, :]).astype(F32)
    token_rank = jnp.sum(selector * rank_sizes.astype(F32)[None, :], axis=1)
    matches = (token_adapter[:, None] == column_owner[None, :]).astype(F32)
    return matches * (ADAPTER_ALPHA / token_rank)[:, None]


def nn(a, b):
    return jnp.dot(a, b, preferred_element_type=F32)


def nt(a, b):
    return lax.dot_general(a, b, (((1,), (1,)), ((), ())), preferred_element_type=F32)


def tn(a, b):
    return lax.dot_general(a, b, (((0,), (0,)), ((), ())), preferred_element_type=F32)


def kernel(
    S, n, D,
    x_hbm, g_hbm, wv_hbm, wo_hbm, at_hbm, up_hbm, gain_hbm, coef_ref,
    gd_ref, gu_ref,
    xs, gs, wv, wo, wa, up, gain, st, s1in, s2out, s2in, agf, agb, ukeep, ikeep, gbuf, gin, gown,
    loc_sem, xsend, xrecv, osend, orecv, rsend, rrecv, dsend, drecv,
    s1_sem, s2send, s2recv, agsend, agrecv, agp_sem, rlsend, rlrecv, gsend, grecv,
):
    sec = lax.axis_index("section")
    f = lax.axis_index("fsdp")
    h = n // 2
    q = f // 2
    c = f % 2
    partner = q * 2 + 1 - c
    rq, dl = xs.shape[2:]
    T = n * rq
    V = up.shape[2]
    packed = at_hbm.shape[0]
    wide = up.shape[1]
    s1 = sec + 1 - 2 * (sec % 2)
    s2 = (sec + 2) % S
    s3 = (s1 + 2) % S

    def rc(src, dst, ssem, rsem, section, fs):
        return pltpu.make_async_remote_copy(
            src_ref=src, dst_ref=dst, send_sem=ssem, recv_sem=rsem,
            device_id=(section, fs), device_id_type=MESH)

    barrier = pltpu.get_barrier_semaphore()
    for k in range(1, n):
        pl.semaphore_signal(barrier, inc=1, device_id=(sec, (f + k) % n), device_id_type=MESH)
    for k in range(1, S):
        pl.semaphore_signal(barrier, inc=1, device_id=((sec + k) % S, f), device_id_type=MESH)
    for r, fill in ((wa, packed), (up, packed)):
        r[:, fill:, :] = jnp.zeros((S, wide - fill, r.shape[2]), r.dtype)
    pl.semaphore_wait(barrier, n - 1 + S - 1)

    pending = []
    local = []

    def own(i, src, slots, rows):
        half = rows // 2
        cp = pltpu.make_async_copy(src, slots.at[sec, pl.ds(0, rows)], loc_sem.at[i])
        cp.start()
        local.append(cp)
        for d, peer, order in ((0, s1, (0, 1)), (1, s2, (1, 0))):
            for b in order:
                r = rc(src.at[pl.ds(b * half, half)], slots.at[sec, pl.ds(b * half, half)],
                       osend.at[i, d, b], orecv.at[i, d, b], peer, f)
                r.start()
                pending.append(r)

    def got(i, slots, rows, d, b, slot):
        half = rows // 2
        ref = slots.at[slot, pl.ds(b * half, half)]
        rc(ref, ref, osend.at[i, d, b], orecv.at[i, d, b], s1, f).wait_recv()
        return ref

    def relay(i, slots, rows):
        for d, slot, peer in ((0, s1, s2), (1, s2, s1)):
            ref = got(i, slots, rows, d, d, slot)
            r = rc(ref, ref, rsend.at[i, d], rrecv.at[i, d], peer, f)
            r.start()
            pending.append(r)

    def finish(i, slots, rows):
        half = rows // 2
        got(i, slots, rows, 0, 1, s1)
        got(i, slots, rows, 1, 0, s2)
        for d in (0, 1):
            ref = slots.at[s3, pl.ds(d * half, half)]
            rc(ref, ref, rsend.at[i, d], rrecv.at[i, d], s1, f).wait_recv()

    def exchange(i, src, dst):
        mine = src.at[pl.ds(sec * rq, rq)]
        cp = pltpu.make_async_copy(mine.at[:, pl.ds(pl.multiple_of(f * dl, LANES), dl)], dst.at[f], loc_sem.at[3 + i])
        cp.start()
        local.append(cp)
        for k in range(1, n):
            p = (f + k) % n
            r = rc(mine.at[:, pl.ds(pl.multiple_of(p * dl, LANES), dl)], dst.at[f],
                   xsend.at[i, k], xrecv.at[i, k], sec, p)
            r.start()
            pending.append(r)

    def exchanged(i, dst):
        for k in range(1, n):
            ref = dst.at[(f + n - k) % n]
            rc(ref, ref, xsend.at[i, k], xrecv.at[i, k], sec, f).wait_recv()

    half_v, half_o = wv.shape[1], wo.shape[1]
    exchange(0, x_hbm, xs.at[0])
    own(0, wv_hbm, wv, half_v)
    own(1, at_hbm, wa, packed)
    for j, (src, slots, rows) in enumerate(((up_hbm, up, packed), (gain_hbm, gain, gain.shape[1]))):
        cp = pltpu.make_async_copy(src, slots.at[sec, pl.ds(0, rows)], loc_sem.at[5 + j])
        cp.start()
        local.append(cp)
        for k in range(1, S):
            r = rc(src, slots.at[sec, pl.ds(0, rows)], dsend.at[j, k], drecv.at[j, k], (sec + k) % S, f)
            r.start()
            pending.append(r)
    exchange(1, g_hbm, gs)
    relay(0, wv, half_v)
    relay(1, wa, packed)
    own(2, wo_hbm, wo, half_o)
    for cp in local:
        cp.wait()
    exchanged(0, xs.at[0])
    finish(0, wv, half_v)
    finish(1, wa, packed)
    for j, (slots, rows) in enumerate(((up, packed), (gain, gain.shape[1]))):
        for k in range(1, S):
            ref = slots.at[(sec + S - k) % S, pl.ds(0, rows)]
            rc(ref, ref, dsend.at[j, k], drecv.at[j, k], sec, f).wait_recv()

    low_col = lax.broadcasted_iota(jnp.int32, (1, wide), 1)

    def scatter(width, between):
        s1c = rc(st.at[:, 1 - c, :, pl.ds(0, width)], s1in.at[:, :, pl.ds(0, width)],
                 s1_sem.at[0], s1_sem.at[1], sec, partner)
        s1c.start()
        between()
        s1c.wait_recv()
        sends = []
        for k in range(1, h):
            to = (q + k) % h
            s2out[k, :, pl.ds(0, width)] = (
                st[to, c, :, pl.ds(0, width)].astype(F32) + s1in[to, :, pl.ds(0, width)].astype(F32)
            ).astype(BF16)
            r = rc(s2out.at[k, :, pl.ds(0, width)], s2in.at[k, :, pl.ds(0, width)],
                   s2send.at[k], s2recv.at[k], sec, to * 2 + c)
            r.start()
            sends.append(r)
        total = st[q, c, :, pl.ds(0, width)].astype(F32) + s1in[q, :, pl.ds(0, width)].astype(F32)
        for k in range(1, h):
            sends[k - 1].wait_recv()
            total = total + s2in[k, :, pl.ds(0, width)].astype(F32)
        s1c.wait_send()
        for r in sends:
            r.wait_send()
        return total

    def gather(buf):
        mine = buf.at[f]
        sends = []
        for k in range(1, h):
            r = rc(mine, mine, agsend.at[k], agrecv.at[k], sec, ((q + k) % h) * 2 + c)
            r.start()
            sends.append(r)
        r = rc(mine, mine, agp_sem.at[0], agp_sem.at[1], sec, partner)
        r.start()
        sends.append(r)
        for k in range(1, h):
            ref = buf.at[((q + h - k) % h) * 2 + c]
            rc(ref, ref, agsend.at[k], agrecv.at[k], sec, partner).wait_recv()
            r = rc(ref, ref, rlsend.at[k], rlrecv.at[k], sec, partner)
            r.start()
            sends.append(r)
        ref = buf.at[partner]
        rc(ref, ref, agp_sem.at[0], agp_sem.at[1], sec, partner).wait_recv()
        for k in range(1, h):
            ref = buf.at[((q + h - k) % h) * 2 + 1 - c]
            rc(ref, ref, rlsend.at[k], rlrecv.at[k], sec, partner).wait_recv()
        for r in sends:
            r.wait_send()

    def gained(l):
        return (xs[l].reshape(T, dl).astype(F32) * gain[l][0:1, :]).astype(BF16)

    def forward(l, carry):
        x32 = xs[l].reshape(T, dl).astype(F32)
        square = jnp.sum(x32 * x32, axis=1, keepdims=True)
        xg = (x32 * gain[l][0:1, :]).astype(BF16)
        st[:, :, :, 0:V] = nn(xg, wv[l]).astype(BF16).reshape(h, 2, rq, V)
        low = jnp.where(low_col == packed, square, nt(xg, wa[l]))
        st[:, :, :, V:V + wide] = low.astype(BF16).reshape(h, 2, rq, wide)
        total = scatter(V + wide, lambda: None)
        tail = total[:, V:]
        mean = jnp.sum(jnp.where(low_col == packed, tail, 0.0), axis=1, keepdims=True) / D
        inv = lax.rsqrt(mean + EPSILON)
        lowp = tail * coef_ref[...]
        value = total[:, :V] * inv + nn((lowp * inv).astype(BF16), up[l])
        ukeep[l] = total
        ikeep[l] = jnp.broadcast_to(inv, (rq, LANES))
        agf[l, f, :, 0:V] = value.astype(BF16)
        agf[l, f, :, V:V + wide] = lowp.astype(BF16)
        gather(agf.at[l])

        @pl.when(l == 0)
        def _():
            relay(2, wo, half_o)
            finish(2, wo, half_o)

        @pl.when(l < S - 1)
        def _():
            out = nn(agf[l, :, :, 0:V].reshape(T, V), wo[l])
            xs[l + 1] = (xs[l].reshape(T, dl).astype(F32) + out).astype(BF16).reshape(n, rq, dl)

        return carry

    before = len(pending)
    lax.fori_loop(0, S, forward, 0)
    late = pending[before:]
    del pending[before:]
    exchanged(1, gs)

    part = V // n

    def gradients(l):
        slot = l % 2
        hv = agb[slot, :, :, 0:V].reshape(T, V)
        hl = agb[slot, :, :, V:V + wide].reshape(T, wide)
        down = tn(hl, gained(l))[:packed]
        row = lax.broadcasted_iota(jnp.int32, (V, LANES), 0)
        col = lax.broadcasted_iota(jnp.int32, (V, LANES), 1)
        pick = jnp.where((row == col + f * part) & (col < part), 1.0, 0.0).astype(BF16)
        cut = nn(hv, pick).astype(BF16)
        upper = tn(agf[l, :, :, V:V + wide].reshape(T, wide), cut)[:packed]

        @pl.when(sec == l)
        def _():
            gown[:, 0:dl] = down
            gown[:, dl:dl + LANES] = upper

        @pl.when(sec != l)
        def _():
            gbuf[l, :, 0:dl] = down.astype(BF16)
            gbuf[l, :, dl:dl + LANES] = upper.astype(BF16)
            rel = (sec - l + S) % S
            rc(gbuf.at[l], gin.at[rel], gsend.at[l], grecv.at[rel], l, f).start()

    def backward(step, carry):
        l = S - 1 - step
        slot = l % 2
        st[:, :, :, 0:V] = nt(gs[...].reshape(T, dl), wo[l]).astype(BF16).reshape(h, 2, rq, V)

        def between():
            @pl.when(step > 0)
            def _():
                gradients(l + 1)

        vg = scatter(V, between).astype(BF16)
        inv = ikeep[l][:, 0:1]
        lg = (nt(vg, up[l]) * coef_ref[...]).astype(BF16)
        u = ukeep[l]
        vg32, lg32 = vg.astype(F32), lg.astype(F32)
        dot = jnp.sum(vg32 * u[:, :V], axis=1, keepdims=True)
        dot = dot + jnp.sum(lg32 * u[:, V:], axis=1, keepdims=True)
        cc = inv * inv * inv * (dot / D)
        high = cc.astype(BF16).astype(F32)
        rest = cc - high
        agb[slot, f, :, 0:V] = (vg32 * inv).astype(BF16)
        tail = jnp.where(low_col == packed, high, jnp.where(low_col == packed + 1, rest, lg32 * inv))
        agb[slot, f, :, V:V + wide] = tail.astype(BF16)
        gather(agb.at[slot])

        @pl.when(l > 0)
        def _():
            hl = agb[slot, :, :, V:V + wide].reshape(T, wide)
            back = nt(agb[slot, :, :, 0:V].reshape(T, V), wv[l]) + nn(hl, wa[l])
            both = (low_col == packed) | (low_col == packed + 1)
            c_all = jnp.sum(jnp.where(both, hl.astype(F32), 0.0), axis=1, keepdims=True)
            new = gs[...].reshape(T, dl).astype(F32) + back * gain[l][0:1, :]
            new = new - c_all * xs[l].reshape(T, dl).astype(F32)
            gs[...] = new.astype(BF16).reshape(n, rq, dl)

        return carry

    lax.fori_loop(0, S, backward, 0)
    gradients(0)

    total = gown[...]
    for k in range(1, S):
        ref = gin.at[k]
        rc(ref, ref, gsend.at[0], grecv.at[k], sec, f).wait_recv()
        total = total + gin[k].astype(F32)
    gu_ref[...] = total[:, dl:dl + part]
    square = jnp.concatenate([total[:, 0:dl], jnp.zeros((wide - packed, dl), F32)], axis=0)
    gd_ref[...] = square.T[:, :packed]
    for r in pending:
        r.wait_send()
    for l in range(S):
        @pl.when(sec != l)
        def _():
            rc(gbuf.at[l], gin.at[1], gsend.at[l], grecv.at[1], l, f).wait_send()
    half = half_o // 2
    for d, slot, peer in ((0, s1, s2), (1, s2, s1)):
        ref = wo.at[slot, pl.ds(d * half, half)]
        rc(ref, ref, rsend.at[2, d], rrecv.at[2, d], peer, f).wait_send()


def local(
    residual_input,
    output_gradient,
    value_projection_weight,
    output_weight,
    adapter_down_weight,
    adapter_up_weight,
    input_norm_scale,
    segment_adapter_index,
    adapter_rank_blocks,
):
    S = lax.axis_size("section")
    n = lax.axis_size("fsdp")
    sec = lax.axis_index("section")
    f = lax.axis_index("fsdp")
    micro, rows, D = residual_input.shape
    V = value_projection_weight.shape[2]
    packed = adapter_down_weight.shape[2]
    wide = -(-packed // (2 * LANES)) * 2 * LANES
    dl = D // n
    R = micro * rows
    rq = R // S
    h = n // 2
    coef = coefficients(segment_adapter_index.reshape(-1), adapter_rank_blocks, wide)
    coef = lax.dynamic_slice_in_dim(coef, sec * rq, rq, 0)
    at = lax.dynamic_slice_in_dim(adapter_down_weight[0], f * dl, dl, 0).T
    gain = jnp.broadcast_to(lax.dynamic_slice_in_dim(input_norm_scale, f * dl, dl, 1), (8, dl))
    W = V + wide
    any_ = pl.BlockSpec(memory_space=pl.ANY)
    vm = pl.BlockSpec(memory_space=pltpu.VMEM)
    DMA = pltpu.SemaphoreType.DMA
    gd, gu = pl.pallas_call(
        functools.partial(kernel, S, n, D),
        out_shape=(
            jax.ShapeDtypeStruct((dl, packed), F32),
            jax.ShapeDtypeStruct((packed, V // n), F32),
        ),
        in_specs=[any_] * 7 + [vm],
        out_specs=(vm, vm),
        scratch_shapes=[
            pltpu.VMEM((S, n, rq, dl), BF16),
            pltpu.VMEM((n, rq, dl), BF16),
            pltpu.VMEM((S, dl, V), BF16),
            pltpu.VMEM((S, V, dl), BF16),
            pltpu.VMEM((S, wide, dl), BF16),
            pltpu.VMEM((S, wide, V), BF16),
            pltpu.VMEM((S, 8, dl), F32),
            pltpu.VMEM((h, 2, rq, W), BF16),
            pltpu.VMEM((h, rq, W), BF16),
            pltpu.VMEM((h, rq, W), BF16),
            pltpu.VMEM((h, rq, W), BF16),
            pltpu.VMEM((S, n, rq, W), BF16),
            pltpu.VMEM((2, n, rq, W), BF16),
            pltpu.VMEM((S, rq, W), F32),
            pltpu.VMEM((S, rq, LANES), F32),
            pltpu.VMEM((S, packed, dl + LANES), BF16),
            pltpu.VMEM((S, packed, dl + LANES), BF16),
            pltpu.VMEM((packed, dl + LANES), F32),
            DMA((7,)), DMA((2, n)), DMA((2, n)),
            DMA((3, 2, 2)), DMA((3, 2, 2)), DMA((3, 2)), DMA((3, 2)),
            DMA((2, S)), DMA((2, S)),
            DMA((2,)), DMA((h,)), DMA((h,)),
            DMA((h,)), DMA((h,)), DMA((2,)), DMA((h,)), DMA((h,)),
            DMA((S,)), DMA((S,)),
        ],
        compiler_params=pltpu.CompilerParams(
            collective_id=0, has_side_effects=True, vmem_limit_bytes=60 * 1024 * 1024
        ),
    )(
        residual_input.reshape(R, D), output_gradient.reshape(R, D),
        value_projection_weight[0], output_weight[0], at, adapter_up_weight[0], gain, coef,
    )
    return (gd[None], gu[None])


def solution(mesh):
    placed = (
        P(None, "fsdp", None),
        P(None, "fsdp", None),
        P("section", "fsdp", None),
        P("section", None, "fsdp"),
        P("section", None, None),
        P("section", None, None),
        P("section", None),
        P(None, "fsdp"),
        P(),
    )
    return jax.shard_map(
        local,
        mesh=mesh,
        in_specs=placed,
        out_specs=(P("section", "fsdp", None), P("section", None, "fsdp")),
        check_vma=False,
    )
```

time: 592 us -> 224 us (0.38); the launches traced: 584 us -> 224 us
  waiting for transfers between devices: 394 us -> 0 us
  Pallas kernels: 0 us -> 214 us
  matrix products: 107 us -> 0 us
  starting transfers between devices: 28.7 us -> 0 us
  other arithmetic: 25.8 us -> 1.7 us
  between operations: 15 us -> 0.66 us
  local copies, waits for them, and re-layouts: 14.2 us -> 7.26 us
    pallas_call x0 -> x1, Pallas kernels: none -> 214 us  [local(): pl.pallas_call(functools.partial(kernel, S, n, D), out_shape=(jax.ShapeDt...]
    ppermute x8 -> x0, waiting for transfers between devices: 158 us -> none  [from_behind(): lax.ppermute(value, axis, [(source, source + steps) for source in range(l...]
    all_gather x2 -> x0, waiting for transfers between devices: 152 us -> none  [the longest x1 76.8 us: local(): out_full = lax.all_gather(output_weight[0], 'fsdp', axis=1, tiled=True)]
    dot_general x33 -> x0, matrix products: 107 us -> none  [the longest x20 56.8 us: contract(): lax.dot_general(left, right, (((left_dim,), (right_dim,)), ((), ())), pre...]
    reduce_scatter x2 -> x0, waiting for transfers between devices: 82.9 us -> none  [the longest x1 60.6 us: local(): lax.psum_scatter(down_sum, 'fsdp', scatter_dimension=0, tiled=True)]
    ppermute x8 -> x0, starting transfers between devices: 28.5 us -> none  [from_behind(): lax.ppermute(value, axis, [(source, source + steps) for source in range(l...]
    dynamic_update_slice x9 -> x0, other arithmetic: 12 us -> none  [remember(): lax.dynamic_update_index_in_dim(stash, jnp.where(active, item, previous),...]
    convert_element_type x4 -> x0, other arithmetic: 10.5 us -> none  [section_backward_pass(): return (input_grad.astype(jnp.bfloat16), low_grad, value_grad)]
  transfers between devices with their start and end apart: 12 -> 0, of which waited for: 12 -> 0; matrix products, arithmetic and copies ran while one was open for 7% -> 0% of each run, Pallas kernels for 0% -> 0%
where the time goes in v1:
time: 224 us
  Pallas kernels  214 us (96%)
  local copies, waits for them, and re-layouts  7.26 us (3%)
    pallas_call x1, Pallas kernels, local(): pl.pallas_call(functools.partial(kernel, S, n, D), out_shape=(jax.ShapeDt...  214 us

profile of v1, /device:TPU:0, one launch (start us, length us, event | category | flops | bytes accessed | tf_op | source)
XLA Modules:
  0.0 224.1 jit_solution(4077902714809454586)
XLA Ops:
  0.6 0.0 copy-start
  0.7 0.9 reshape.46
  1.6 0.7 multiply_bitcast_fusion
  2.2 0.2 reduce-window.8
  2.4 0.1 convert_reduce_fusion
  2.5 0.1 broadcast_in_dim.24
  2.6 0.1 eq.28
  2.6 0.1 select_reduce_fusion
  2.7 0.1 dynamic-slice.1
  2.8 0.1 dynamic-slice.2
  2.9 0.7 constant_dynamic-slice_fusion
  3.6 0.6 broadcast_in_dim.11.gain_hbm
  4.2 0.7 compare_select_fusion.coef_ref
  4.9 0.0 copy-done
  4.9 0.8 dynamic-slice_bitcast_fusion.at_hbm
  5.6 214.4 %shard_map.104 = (f32[1024,160]{1,0:T(8,128)}, f32[160,64]{1,0:T(8,128)}) custom-call(bf16[128,8192]{1,0:T(8,128)(2,1)} %bitcast.15, bf16[128,8192]{1,0:T(8,128)(2,1)} %bitcast.16, bf16[1024,512]{1,0:T(8,128)(2,1)} %bitcast.18, bf16[512,1024]{1,0:T(8,128)(2,1)} %bitcast.19, bf16[160,1024]{1,0:T(8,128)(2,1)} %dynamic-slice_bitcast_fusion.at_hbm, ...), custom_call_target="tpu_custom_call" | custom-call | tf_op jit(solution)/shard_map/pallas_call | solution.py:367
  220.1 2.4 %copy.13 = f32[1,1024,160]{1,2,0:T(8,128)} copy(f32[1,1024,160]{2,1,0:T(8,128)} %bitcast.17) | data formatting | bytes 1310720
  222.5 1.6 copy.14
  (1 shorter events, 0.0 us)
Async XLA Ops:
  0.6 4.3 %copy-start = (bf16[1,8192,160]{1,2,0:T(8,128)(2,1)S(1)}, bf16[1,8192,160]{1,2,0:T(8,128)(2,1)}, u32[]{:S(2)}) copy-start(bf16[1,8192,160]{1,2,0:T(8,128)(2,1)} %param.13) | copy-start | bytes 7864324

commit v2 on v1

v2 whole, which is shorter than its diff:
```python
import functools

import jax
import jax.numpy as jnp
from jax import lax
from jax.experimental import pallas as pl
from jax.experimental.pallas import tpu as pltpu
from jax.sharding import PartitionSpec as P

SEG = 32
EPSILON = 1e-06
ADAPTER_ALPHA = 32.0
LANES = 128
MESH = pl.DeviceIdType.MESH
F32 = jnp.float32
BF16 = jnp.bfloat16


def nn(a, b):
    return jnp.dot(a, b, preferred_element_type=F32)


def nt(a, b):
    return lax.dot_general(a, b, (((1,), (1,)), ((), ())), preferred_element_type=F32)


def tn(a, b):
    return lax.dot_general(a, b, (((0,), (0,)), ((), ())), preferred_element_type=F32)


def kernel(
    S, n, D,
    x_hbm, g_hbm, wv_hbm, wo_hbm, at_hbm, up_hbm, gain_hbm, seg_ref, rank_ref,
    gd_ref, gu_ref,
    xs, gs, wv, wo, wa, up, gain, st, s1in, s2out, s2in, agf, agb, ukeep, ikeep, gbuf, gin, gown, coef_ref,
    loc_sem, xsend, xrecv, osend, orecv, rsend, rrecv, dsend, drecv,
    s1_sem, s2send, s2recv, agsend, agrecv, agp_sem, rlsend, rlrecv, gsend, grecv,
):
    sec = lax.axis_index("section")
    f = lax.axis_index("fsdp")
    h = n // 2
    q = f // 2
    c = f % 2
    partner = q * 2 + 1 - c
    rq, dl = xs.shape[2:]
    T = n * rq
    V = up.shape[2]
    packed = at_hbm.shape[0]
    wide = up.shape[1]
    s1 = sec + 1 - 2 * (sec % 2)
    s2 = (sec + 2) % S
    s3 = (s1 + 2) % S

    def rc(src, dst, ssem, rsem, section, fs):
        return pltpu.make_async_remote_copy(
            src_ref=src, dst_ref=dst, send_sem=ssem, recv_sem=rsem,
            device_id=(section, fs), device_id_type=MESH)

    adapters = rank_ref.shape[0]
    per = seg_ref.shape[1]
    column = lax.broadcasted_iota(jnp.int32, (SEG, wide), 1)
    for j in range(rq // SEG):
        spot = sec * (rq // SEG) + j
        mine = seg_ref[spot // per, spot % per]
        begin, size = jnp.int32(0), jnp.int32(0)
        for a in range(adapters):
            rank = 8 * rank_ref[a]
            begin = begin + jnp.where(mine > a, rank, 0)
            size = size + jnp.where(mine == a, rank, 0)
        inside = (column >= begin) & (column < begin + size)
        scale = ADAPTER_ALPHA / jnp.full((SEG, wide), size, jnp.int32).astype(F32)
        coef_ref[j * SEG:(j + 1) * SEG, :] = jnp.where(inside, scale, 0.0)

    barrier = pltpu.get_barrier_semaphore()
    for k in range(1, n):
        pl.semaphore_signal(barrier, inc=1, device_id=(sec, (f + k) % n), device_id_type=MESH)
    for k in range(1, S):
        pl.semaphore_signal(barrier, inc=1, device_id=((sec + k) % S, f), device_id_type=MESH)
    for r, fill in ((wa, packed), (up, packed)):
        r[:, fill:, :] = jnp.zeros((S, wide - fill, r.shape[2]), r.dtype)
    pl.semaphore_wait(barrier, n - 1 + S - 1)

    pending = []
    local = []

    arrays = (
        (wv_hbm, wv, wv.shape[1]), (at_hbm, wa, packed), (wo_hbm, wo, wo.shape[1]), (up_hbm, up, packed)
    )
    peers = (s1, s2)

    def piece(i, d, b):
        src, slots, rows = arrays[i]
        half = rows // 2
        return rc(src.at[pl.ds(b * half, half)], slots.at[sec, pl.ds(b * half, half)],
                  osend.at[i, d, b], orecv.at[i, d, b], peers[d], f)

    def passed(i, d):
        _, slots, rows = arrays[i]
        half = rows // 2
        ref = slots.at[peers[d], pl.ds(d * half, half)]
        return rc(ref, ref, rsend.at[i, d], rrecv.at[i, d], peers[1 - d], f)

    def keep(i):
        src, slots, rows = arrays[i]
        cp = pltpu.make_async_copy(src, slots.at[sec, pl.ds(0, rows)], loc_sem.at[i])
        cp.start()
        local.append(cp)

    def first(i):
        for d in (0, 1):
            piece(i, d, d).start()

    def second(i):
        for d in (0, 1):
            piece(i, d, 1 - d).start()

    def got(i, d, b):
        _, slots, rows = arrays[i]
        half = rows // 2
        ref = slots.at[peers[d], pl.ds(b * half, half)]
        rc(ref, ref, osend.at[i, d, b], orecv.at[i, d, b], peers[d], f).wait_recv()

    def relay(i):
        for d in (0, 1):
            got(i, d, d)
            passed(i, d).start()

    def arrive(i, l):
        _, slots, rows = arrays[i]
        half = rows // 2
        for d in (0, 1):
            @pl.when(l == peers[d])
            def _():
                got(i, d, 1 - d)

        @pl.when(l == s3)
        def _():
            for d in (0, 1):
                ref = slots.at[s3, pl.ds(d * half, half)]
                rc(ref, ref, rsend.at[i, d], rrecv.at[i, d], s1, f).wait_recv()

    def exchange(i, src, dst):
        mine = src.at[pl.ds(sec * rq, rq)]
        cp = pltpu.make_async_copy(mine.at[:, pl.ds(pl.multiple_of(f * dl, LANES), dl)], dst.at[f], loc_sem.at[4 + i])
        cp.start()
        local.append(cp)
        for k in range(1, n):
            p = (f + k) % n
            r = rc(mine.at[:, pl.ds(pl.multiple_of(p * dl, LANES), dl)], dst.at[f],
                   xsend.at[i, k], xrecv.at[i, k], sec, p)
            r.start()
            pending.append(r)

    def exchanged(i, dst):
        for k in range(1, n):
            ref = dst.at[(f + n - k) % n]
            rc(ref, ref, xsend.at[i, k], xrecv.at[i, k], sec, f).wait_recv()

    outer = (sec == 0) | (sec == S - 1)
    exchange(0, x_hbm, xs.at[0])
    for i in (0, 1, 3):
        first(i)

    @pl.when(outer)
    def _():
        for i in (0, 1, 3):
            second(i)
        first(2)
        second(2)

    for i in range(4):
        keep(i)
    cp = pltpu.make_async_copy(gain_hbm, gain.at[sec], loc_sem.at[6])
    cp.start()
    local.append(cp)
    for k in range(1, S):
        r = rc(gain_hbm, gain.at[sec], dsend.at[k], drecv.at[k], (sec + k) % S, f)
        r.start()
        pending.append(r)
    exchange(1, g_hbm, gs)
    for i in (0, 1, 3):
        relay(i)

    @pl.when(jnp.logical_not(outer))
    def _():
        for i in (0, 1, 3):
            second(i)
        relay(2)
        first(2)
        second(2)

    for cp in local:
        cp.wait()
    exchanged(0, xs.at[0])
    for k in range(1, S):
        ref = gain.at[(sec + S - k) % S]
        rc(ref, ref, dsend.at[k], drecv.at[k], sec, f).wait_recv()

    low_col = lax.broadcasted_iota(jnp.int32, (1, wide), 1)

    def scatter(width, t, early, between):
        s1c = rc(st.at[:, 1 - c, :, pl.ds(0, width)], s1in.at[t, :, :, pl.ds(0, width)],
                 s1_sem.at[t, 0], s1_sem.at[t, 1], sec, partner)
        s1c.start()
        early()
        s1c.wait_recv()
        sends = []
        for k in range(1, h):
            to = (q + k) % h
            s2out[k, :, pl.ds(0, width)] = (
                st[to, c, :, pl.ds(0, width)].astype(F32) + s1in[t, to, :, pl.ds(0, width)].astype(F32)
            ).astype(BF16)
            r = rc(s2out.at[k, :, pl.ds(0, width)], s2in.at[t, k, :, pl.ds(0, width)],
                   s2send.at[t, k], s2recv.at[t, k], sec, to * 2 + c)
            r.start()
            sends.append(r)
        between()
        total = st[q, c, :, pl.ds(0, width)].astype(F32) + s1in[t, q, :, pl.ds(0, width)].astype(F32)
        for k in range(1, h):
            sends[k - 1].wait_recv()
            total = total + s2in[t, k, :, pl.ds(0, width)].astype(F32)
        s1c.wait_send()
        for r in sends:
            r.wait_send()
        return total

    def gather(buf, t):
        mine = buf.at[f]
        sends = []
        for k in range(1, h):
            r = rc(mine, mine, agsend.at[t, k], agrecv.at[t, k], sec, ((q + k) % h) * 2 + c)
            r.start()
            sends.append(r)
        r = rc(mine, mine, agp_sem.at[t, 0], agp_sem.at[t, 1], sec, partner)
        r.start()
        sends.append(r)
        for k in range(1, h):
            ref = buf.at[((q + h - k) % h) * 2 + c]
            rc(ref, ref, agsend.at[t, k], agrecv.at[t, k], sec, partner).wait_recv()
            r = rc(ref, ref, rlsend.at[t, k], rlrecv.at[t, k], sec, partner)
            r.start()
            sends.append(r)
        ref = buf.at[partner]
        rc(ref, ref, agp_sem.at[t, 0], agp_sem.at[t, 1], sec, partner).wait_recv()
        for k in range(1, h):
            ref = buf.at[((q + h - k) % h) * 2 + 1 - c]
            rc(ref, ref, rlsend.at[t, k], rlrecv.at[t, k], sec, partner).wait_recv()
        for r in sends:
            r.wait_send()

    def gained(l):
        return (xs[l].reshape(T, dl).astype(F32) * gain[l][0:1, :]).astype(BF16)

    def forward(l, carry):
        for i in (0, 1, 3):
            arrive(i, l)
        x32 = xs[l].reshape(T, dl).astype(F32)
        square = jnp.sum(x32 * x32, axis=1, keepdims=True)
        xg = (x32 * gain[l][0:1, :]).astype(BF16)
        st[:, :, :, 0:V] = nn(xg, wv[l]).astype(BF16).reshape(h, 2, rq, V)
        low = jnp.where(low_col == packed, square, nt(xg, wa[l]))
        st[:, :, :, V:V + wide] = low.astype(BF16).reshape(h, 2, rq, wide)
        total = scatter(V + wide, 0, lambda: None, lambda: None)
        tail = total[:, V:]
        mean = jnp.sum(jnp.where(low_col == packed, tail, 0.0), axis=1, keepdims=True) / D
        inv = lax.rsqrt(mean + EPSILON)
        lowp = tail * coef_ref[...]
        value = total[:, :V] * inv + nn((lowp * inv).astype(BF16), up[l])
        ukeep[l] = total
        ikeep[l] = jnp.broadcast_to(inv, (rq, LANES))
        agf[l, f, :, 0:V] = value.astype(BF16)
        agf[l, f, :, V:V + wide] = lowp.astype(BF16)

        @pl.when(l < S - 1)
        def _():
            gather(agf.at[l], 0)

        @pl.when((l == 0) & outer)
        def _():
            relay(2)

        arrive(2, l)

        @pl.when(l < S - 1)
        def _():
            out = nn(agf[l, :, :, 0:V].reshape(T, V), wo[l])
            xs[l + 1] = (xs[l].reshape(T, dl).astype(F32) + out).astype(BF16).reshape(n, rq, dl)

        return carry

    lax.fori_loop(0, S, forward, 0)
    exchanged(1, gs)

    part = V // n

    def gradients(l):
        slot = l % 2
        hv = agb[slot, :, :, 0:V].reshape(T, V)
        hl = agb[slot, :, :, V:V + wide].reshape(T, wide)
        down = tn(hl, gained(l))[:packed]
        row = lax.broadcasted_iota(jnp.int32, (V, LANES), 0)
        col = lax.broadcasted_iota(jnp.int32, (V, LANES), 1)
        pick = jnp.where((row == col + f * part) & (col < part), 1.0, 0.0).astype(BF16)
        cut = nn(hv, pick).astype(BF16)
        upper = tn(agf[l, :, :, V:V + wide].reshape(T, wide), cut)[:packed]

        @pl.when(sec == l)
        def _():
            gown[:, 0:dl] = down
            gown[:, dl:dl + LANES] = upper

        @pl.when(sec != l)
        def _():
            gbuf[l, :, 0:dl] = down.astype(BF16)
            gbuf[l, :, dl:dl + LANES] = upper.astype(BF16)
            rel = (sec - l + S) % S
            rc(gbuf.at[l], gin.at[rel], gsend.at[l], grecv.at[rel], l, f).start()

    def backward(step, carry):
        l = S - 1 - step
        slot = l % 2
        st[:, :, :, 0:V] = nt(gs[...].reshape(T, dl), wo[l]).astype(BF16).reshape(h, 2, rq, V)

        def between():
            @pl.when(step == 0)
            def _():
                gather(agf.at[S - 1], 1)

            @pl.when(step > 0)
            def _():
                gradients(l + 1)

        vg = scatter(V, 1, lambda: None, between).astype(BF16)
        inv = ikeep[l][:, 0:1]
        lg = (nt(vg, up[l]) * coef_ref[...]).astype(BF16)
        u = ukeep[l]
        vg32, lg32 = vg.astype(F32), lg.astype(F32)
        dot = jnp.sum(vg32 * u[:, :V], axis=1, keepdims=True)
        dot = dot + jnp.sum(lg32 * u[:, V:], axis=1, keepdims=True)
        cc = inv * inv * inv * (dot / D)
        high = cc.astype(BF16).astype(F32)
        rest = cc - high
        agb[slot, f, :, 0:V] = (vg32 * inv).astype(BF16)
        tail = jnp.where(low_col == packed, high, jnp.where(low_col == packed + 1, rest, lg32 * inv))
        agb[slot, f, :, V:V + wide] = tail.astype(BF16)
        gather(agb.at[slot], 0)

        @pl.when(l > 0)
        def _():
            hl = agb[slot, :, :, V:V + wide].reshape(T, wide)
            back = nt(agb[slot, :, :, 0:V].reshape(T, V), wv[l]) + nn(hl, wa[l])
            both = (low_col == packed) | (low_col == packed + 1)
            c_all = jnp.sum(jnp.where(both, hl.astype(F32), 0.0), axis=1, keepdims=True)
            new = gs[...].reshape(T, dl).astype(F32) + back * gain[l][0:1, :]
            new = new - c_all * xs[l].reshape(T, dl).astype(F32)
            gs[...] = new.astype(BF16).reshape(n, rq, dl)

        return carry

    lax.fori_loop(0, S, backward, 0)
    gradients(0)

    total = gown[...]
    for k in range(1, S):
        ref = gin.at[k]
        rc(ref, ref, gsend.at[0], grecv.at[k], sec, f).wait_recv()
        total = total + gin[k].astype(F32)
    gu_ref[...] = total[:, dl:dl + part]
    square = jnp.concatenate([total[:, 0:dl], jnp.zeros((wide - packed, dl), F32)], axis=0)
    gd_ref[...] = square.T[:, :packed]
    for r in pending:
        r.wait_send()
    for l in range(S):
        @pl.when(sec != l)
        def _():
            rc(gbuf.at[l], gin.at[1], gsend.at[l], grecv.at[1], l, f).wait_send()
    for i in range(4):
        for d in (0, 1):
            piece(i, d, 0).wait_send()
            piece(i, d, 1).wait_send()
            passed(i, d).wait_send()


def local(
    residual_input,
    output_gradient,
    value_projection_weight,
    output_weight,
    adapter_down_weight,
    adapter_up_weight,
    input_norm_scale,
    segment_adapter_index,
    adapter_rank_blocks,
):
    S = lax.axis_size("section")
    n = lax.axis_size("fsdp")
    f = lax.axis_index("fsdp")
    micro, rows, D = residual_input.shape
    V = value_projection_weight.shape[2]
    packed = adapter_down_weight.shape[2]
    wide = -(-packed // (2 * LANES)) * 2 * LANES
    dl = D // n
    R = micro * rows
    rq = R // S
    h = n // 2
    at = lax.dynamic_slice_in_dim(adapter_down_weight[0], f * dl, dl, 0).T
    gain = jnp.broadcast_to(lax.dynamic_slice_in_dim(input_norm_scale, f * dl, dl, 1), (8, dl))
    W = V + wide
    any_ = pl.BlockSpec(memory_space=pl.ANY)
    vm = pl.BlockSpec(memory_space=pltpu.VMEM)
    sm = pl.BlockSpec(memory_space=pltpu.SMEM)
    DMA = pltpu.SemaphoreType.DMA
    gd, gu = pl.pallas_call(
        functools.partial(kernel, S, n, D),
        out_shape=(
            jax.ShapeDtypeStruct((dl, packed), F32),
            jax.ShapeDtypeStruct((packed, V // n), F32),
        ),
        in_specs=[any_] * 7 + [sm, sm],
        out_specs=(vm, vm),
        scratch_shapes=[
            pltpu.VMEM((S, n, rq, dl), BF16),
            pltpu.VMEM((n, rq, dl), BF16),
            pltpu.VMEM((S, dl, V), BF16),
            pltpu.VMEM((S, V, dl), BF16),
            pltpu.VMEM((S, wide, dl), BF16),
            pltpu.VMEM((S, wide, V), BF16),
            pltpu.VMEM((S, 8, dl), F32),
            pltpu.VMEM((h, 2, rq, W), BF16),
            pltpu.VMEM((2, h, rq, W), BF16),
            pltpu.VMEM((h, rq, W), BF16),
            pltpu.VMEM((2, h, rq, W), BF16),
            pltpu.VMEM((S, n, rq, W), BF16),
            pltpu.VMEM((2, n, rq, W), BF16),
            pltpu.VMEM((S, rq, W), F32),
            pltpu.VMEM((S, rq, LANES), F32),
            pltpu.VMEM((S, packed, dl + LANES), BF16),
            pltpu.VMEM((S, packed, dl + LANES), BF16),
            pltpu.VMEM((packed, dl + LANES), F32),
            pltpu.VMEM((rq, wide), F32),
            DMA((7,)), DMA((2, n)), DMA((2, n)),
            DMA((4, 2, 2)), DMA((4, 2, 2)), DMA((4, 2)), DMA((4, 2)),
            DMA((S,)), DMA((S,)),
            DMA((2, 2)), DMA((2, h)), DMA((2, h)),
            DMA((2, h)), DMA((2, h)), DMA((2, 2)), DMA((2, h)), DMA((2, h)),
            DMA((S,)), DMA((S,)),
        ],
        compiler_params=pltpu.CompilerParams(
            collective_id=0, has_side_effects=True, vmem_limit_bytes=60 * 1024 * 1024
        ),
    )(
        residual_input.reshape(R, D), output_gradient.reshape(R, D),
        value_projection_weight[0], output_weight[0], at, adapter_up_weight[0], gain,
        segment_adapter_index, adapter_rank_blocks,
    )
    return (gd[None], gu[None])


def solution(mesh):
    placed = (
        P(None, "fsdp", None),
        P(None, "fsdp", None),
        P("section", "fsdp", None),
        P("section", None, "fsdp"),
        P("section", None, None),
        P("section", None, None),
        P("section", None),
        P(None, "fsdp"),
        P(),
    )
    return jax.shard_map(
        local,
        mesh=mesh,
        in_specs=placed,
        out_specs=(P("section", "fsdp", None), P("section", None, "fsdp")),
        check_vma=False,
    )
```

time: 224 us -> 208 us (0.929)
  Pallas kernels: 214 us -> 200 us
    pallas_call x1, Pallas kernels: 214 us -> 200 us  [local(): pl.pallas_call(functools.partial(kernel, S, n, D), out_shape=(jax.ShapeDt...]
where the time goes in v2:
time: 208 us; the launch traced here: 207 us
  Pallas kernels  200 us (96%)
  local copies, waits for them, and re-layouts  6.47 us (3%)
    pallas_call x1, Pallas kernels, local(): pl.pallas_call(functools.partial(kernel, S, n, D), out_shape=(jax.ShapeDt...  200 us
    unnamed x4, local copies, waits for them, and re-layouts  4.26 us

profile of v2, /device:TPU:0, one launch (start us, length us, event | category | flops | bytes accessed | tf_op | source)
XLA Modules:
  0.0 207.3 jit_solution(10688526764947305909)
XLA Ops:
  0.6 0.0 copy-start
  0.6 0.8 constant_dynamic-slice_fusion
  1.5 0.6 broadcast_in_dim.14.gain_hbm
  2.1 0.3 copy-done
  2.4 0.8 dynamic-slice_bitcast_fusion.at_hbm
  3.1 200.2 %shard_map.104 = (f32[1024,160]{1,0:T(8,128)}, f32[160,64]{1,0:T(8,128)}) custom-call(bf16[128,8192]{1,0:T(8,128)(2,1)} %bitcast.12, bf16[128,8192]{1,0:T(8,128)(2,1)} %bitcast.13, bf16[1024,512]{1,0:T(8,128)(2,1)} %bitcast.15, bf16[512,1024]{1,0:T(8,128)(2,1)} %bitcast.16, bf16[160,1024]{1,0:T(8,128)(2,1)} %dynamic-slice_bitcast_fusion.at_hbm, ...), custom_call_target="tpu_custom_call" | custom-call | tf_op jit(solution)/shard_map/pallas_call | solution.py:413
  203.4 2.4 %copy.11 = f32[1,1024,160]{1,2,0:T(8,128)} copy(f32[1,1024,160]{2,1,0:T(8,128)} %bitcast.14) | data formatting | bytes 1310720
  205.8 1.6 copy.12
Async XLA Ops:
  0.6 1.8 copy-start
